TPU v7x, 256 devices: a whole 4x4x8 slice. The times are simulated.
256 devices in a mesh: strip: 16 (over z, core), sample: 16 (over y, x).
Axes of the slice: x: 4, y: 4, z: 8, core: 2. Of those that a mesh axis runs over, the one named last changes fastest.
Arguments:
- images: bfloat16 [16, 48, 108, 2048], P('sample', 'strip'), may hold values from -36 to 36
- w_point: bfloat16 [2048, 256], P('sample'), may hold values from -0.125 to 0.125
- w_atrous: bfloat16 [2048, 2304], P('sample'), may hold values from -0.046875 to 0.046875
- w_image: bfloat16 [2048, 256], P('sample'), may hold values from -0.125 to 0.125
- w_proj: bfloat16 [768, 256], P('sample'), may hold values from -0.21875 to 0.21875
- cotangent: bfloat16 [16, 48, 108, 256], P('sample', 'strip'), may hold values from -6 to 6
Outputs:
- result: bfloat16 [16, 48, 108, 256], P('sample', 'strip')
- input_grad: bfloat16 [16, 48, 108, 2048], P('sample', 'strip')
- grad_point: float32 [2048, 256], P('sample')
- grad_atrous: float32 [2048, 2304], P('sample')
- grad_image: float32 [2048, 256], P('sample')
- grad_proj: float32 [768, 256], P('sample')
All inputs are finite; a program needn't handle non-finite values.
Results may differ from a plain program's by a relative error of at most 0.038.
Values may be sent and summed in bfloat16 or wider, within the bound.
A program may use at most 128 MiB of HBM per device.

v0:
```python
import jax
import jax.numpy as jnp
from jax import lax
from jax.sharding import Mesh
from jax.sharding import PartitionSpec as P

DILATION_RATE = 12
STRIP_SAMPLE = ("strip_0", "strip_1", "sample_0", "sample_1")
STRIP = ("strip_0", "strip_1")
SAMPLE = ("sample_0", "sample_1")
EPSILON = 1e-05


def one_axis_at_a_time(array, axes):
    for axis in axes:
        array = lax.psum(array, axis)
    return array


def side_by_side(arrays, axis, dim, along):
    widths = [a.shape[along] for a in arrays]
    both = jnp.concatenate(arrays, axis=along)
    filled = lax.all_gather(both, axis, axis=dim, tiled=True)
    return tuple(jnp.split(filled, [sum(widths[:k]) for k in range(1, len(widths))], axis=along))


def from_everyone(array, axis):
    peers = lax.axis_size(axis)
    return lax.all_to_all(
        jnp.broadcast_to(array[None], (peers, *array.shape)), axis, 0, 0, tiled=True
    )


def taken_together(array, axis):
    return from_everyone(array, axis).sum(axis=0)


def passed_along(array, axis, by):
    peers = lax.axis_size(axis)
    pairs = [(i, i + by) for i in range(peers) if 0 <= i + by < peers]
    return lax.ppermute(array, axis, pairs)


def cut_along(array, dim, peers):
    before, after = (array.shape[:dim], array.shape[dim + 1 :])
    return jnp.moveaxis(array.reshape(*before, peers, -1, *after), dim, 0)


def sum_at_owner(array, axis, dim):
    tiles = cut_along(array, dim, lax.axis_size(axis))
    arrived = lax.all_to_all(tiles, axis, split_axis=0, concat_axis=0, tiled=True)
    return arrived.astype(jnp.float32).sum(axis=0)


def joined_along(tiles, dim):
    lengths = list(tiles.shape[1:])
    lengths[dim] *= tiles.shape[0]
    return jnp.moveaxis(tiles, 0, dim).reshape(lengths)


def gather_directly(array, axis, dim):
    tiles = from_everyone(array, axis)
    return joined_along(tiles, dim)


def total_of_pieces(array, axis):
    return lax.all_gather(array, axis).astype(jnp.float32).sum(0)


def shifted_axis(values, offset, axis_dim):
    if offset == 0:
        return values
    length = values.shape[axis_dim]
    margin = abs(offset)
    pad_widths = [(0, 0)] * values.ndim
    pad_widths[axis_dim] = (margin, margin)
    padded = jnp.pad(values, pad_widths)
    return lax.slice_in_dim(padded, margin + offset, margin + offset + length, axis=axis_dim)


def contract_last(left, right):
    return lax.dot_general(
        left, right, (((left.ndim - 1,), (1,)), ((), ())), preferred_element_type=jnp.float32
    )


def swish(values):
    return values * jax.nn.sigmoid(values)


def swish_slope(values):
    sigma = jax.nn.sigmoid(values)
    return sigma * (1.0 + values * (1.0 - sigma))


def row_part(source, tap_rows, out_width):
    tap_product = jnp.dot(source, tap_rows, preferred_element_type=jnp.float32)
    summed_terms = jnp.zeros(tap_product.shape[:-1] + (out_width,), jnp.float32)
    for column_stride in (-1, 0, 1):
        kernel_tap_slice = tap_product[
            ..., (column_stride + 1) * out_width : (column_stride + 2) * out_width
        ]
        summed_terms = summed_terms + shifted_axis(
            kernel_tap_slice, DILATION_RATE * column_stride, 1
        )
    return summed_terms


def column_stack(gradient_list):
    return jnp.concatenate(
        [
            shifted_axis(gradient_list, -DILATION_RATE * column_stride, 1)
            for column_stride in (-1, 0, 1)
        ],
        -1,
    )


def moments(values, position_count):
    branch_sums = jnp.stack([jnp.sum(tensor, axis=(0, 1)) for tensor in values])
    squares = jnp.stack([jnp.sum(jnp.square(tensor), axis=(0, 1)) for tensor in values])
    totals, powers = (
        one_axis_at_a_time(branch_sums, STRIP_SAMPLE),
        one_axis_at_a_time(squares, STRIP_SAMPLE),
    )
    centres = totals / position_count
    variances = powers / position_count - jnp.square(centres)
    return (centres, variances)


def on_device(images, w_point, w_atrous, w_image, w_proj, cotangent):
    sample_map = images[0]
    strip_row_count, col_count, chan_count = sample_map.shape
    out_width = w_point.shape[1]
    tap_band = 3 * out_width
    strips = lax.axis_size(STRIP)
    samples = lax.axis_size(SAMPLE)
    map_area = strips * strip_row_count * col_count
    position_count = samples * map_area
    strip_extent = DILATION_RATE // strip_row_count
    factor = 1.0 / samples
    point_full, atrous_full, image_full, proj_full = (
        *side_by_side((w_point, w_atrous, w_image), SAMPLE, 0, 1),
        lax.all_gather(w_proj, SAMPLE, axis=0, tiled=True),
    )
    pool_total = taken_together(jnp.sum(sample_map, axis=(0, 1), dtype=jnp.float32), STRIP)
    pooled = (pool_total / map_area).astype(jnp.bfloat16)

    def tap_rows(row_stride):
        return atrous_full[:, (row_stride + 1) * tap_band : (row_stride + 2) * tap_band]

    point_out = jnp.dot(sample_map, point_full, preferred_element_type=jnp.float32)
    dilated_branch_output = row_part(sample_map, tap_rows(0), out_width)
    for row_stride in (1, -1):
        remote = passed_along(sample_map, STRIP, -row_stride * strip_extent)
        dilated_branch_output = dilated_branch_output + row_part(
            remote, tap_rows(row_stride), out_width
        )
    centres, variances = moments([point_out, dilated_branch_output], position_count)
    scales = lax.rsqrt(variances + EPSILON)
    norm_point = (point_out - centres[0]) * scales[0]
    norm_atrous = (dilated_branch_output - centres[1]) * scales[1]
    relu_joined = jnp.concatenate(
        [swish(norm_point).astype(jnp.bfloat16), swish(norm_atrous).astype(jnp.bfloat16)], -1
    )
    image_out = jnp.dot(pooled, image_full, preferred_element_type=jnp.float32)
    layer_mean = jnp.mean(image_out)
    layer_spread = jnp.mean(jnp.square(image_out - layer_mean))
    layer_scale = lax.rsqrt(layer_spread + EPSILON)
    layer_norm = (image_out - layer_mean) * layer_scale
    relu_image = swish(layer_norm).astype(jnp.bfloat16)
    mixed_out = jnp.dot(relu_joined, proj_full[: 2 * out_width], preferred_element_type=jnp.float32)
    mixed_out = mixed_out + jnp.dot(
        relu_image, proj_full[2 * out_width :], preferred_element_type=jnp.float32
    )
    mix_centre, mix_spread = moments([mixed_out], position_count)
    mix_scale = lax.rsqrt(mix_spread[0] + EPSILON)
    norm_mix = (mixed_out - mix_centre[0]) * mix_scale
    result = swish(norm_mix).astype(jnp.bfloat16)
    upstream = cotangent[0].astype(jnp.float32) * swish_slope(norm_mix)
    first_sum, second_sum = (
        one_axis_at_a_time(jnp.sum(upstream, axis=(0, 1)), STRIP_SAMPLE),
        one_axis_at_a_time(jnp.sum(upstream * norm_mix, axis=(0, 1)), STRIP_SAMPLE),
    )
    grad_mix = (
        upstream - first_sum / position_count - norm_mix * (second_sum / position_count)
    ) * mix_scale
    grad_mix_b = grad_mix.astype(jnp.bfloat16)
    column_total = taken_together(jnp.sum(grad_mix, axis=(0, 1)), STRIP)
    column_b = column_total.astype(jnp.bfloat16)
    back_joined = contract_last(grad_mix_b, proj_full[: 2 * out_width])
    back_image = contract_last(column_b, proj_full[2 * out_width :])
    up_image = back_image * swish_slope(layer_norm)
    grad_image_b = (
        (up_image - jnp.mean(up_image) - layer_norm * jnp.mean(up_image * layer_norm)) * layer_scale
    ).astype(jnp.bfloat16)
    grad_pool = contract_last(grad_image_b, image_full)
    up_point = back_joined[..., :out_width] * swish_slope(norm_point)
    up_atrous = back_joined[..., out_width:] * swish_slope(norm_atrous)
    local_sums = jnp.stack(
        [
            jnp.sum(up_point, axis=(0, 1)),
            jnp.sum(up_point * norm_point, axis=(0, 1)),
            jnp.sum(up_atrous, axis=(0, 1)),
            jnp.sum(up_atrous * norm_atrous, axis=(0, 1)),
        ]
    )
    branch_means = one_axis_at_a_time(local_sums, STRIP_SAMPLE) / position_count
    grad_point_b = ((up_point - branch_means[0] - norm_point * branch_means[1]) * scales[0]).astype(
        jnp.bfloat16
    )
    grad_atrous_b = (
        (up_atrous - branch_means[2] - norm_atrous * branch_means[3]) * scales[1]
    ).astype(jnp.bfloat16)
    input_grad = contract_last(grad_point_b, point_full) + grad_pool / map_area
    column_sets = []
    for row_stride in (-1, 0, 1):
        if row_stride == 0:
            source = grad_atrous_b
        else:
            source = passed_along(grad_atrous_b, STRIP, row_stride * strip_extent)
        stacked = column_stack(source)
        column_sets.append(stacked)
        input_grad = input_grad + contract_last(stacked, tap_rows(row_stride))
    image_gate = jnp.where(lax.axis_index(STRIP) == 0, 1.0, 0.0).astype(jnp.float32)
    columns_all = jnp.concatenate([grad_point_b] + column_sets, -1).reshape(
        strip_row_count * col_count, 10 * out_width
    )
    flat_map = sample_map.reshape(strip_row_count * col_count, chan_count)
    image_cols = grad_image_b.astype(jnp.float32) * (image_gate * factor)
    pooled_wide = pooled.astype(jnp.float32)
    proj_local = (
        lax.dot_general(
            relu_joined.reshape(-1, 2 * out_width),
            grad_mix_b.reshape(-1, out_width),
            (((0,), (0,)), ((), ())),
            preferred_element_type=jnp.float32,
        )
        * factor
    )
    proj_image = (
        relu_image.astype(jnp.float32)[:, None]
        * (column_b.astype(jnp.float32) * (image_gate * factor))[None, :]
    )
    proj_shard = sum_at_owner(
        jnp.concatenate([proj_local, proj_image], 0).astype(jnp.bfloat16), SAMPLE, 0
    )
    chan_piece = chan_count // (samples * strips)
    swapped_map = (
        flat_map.reshape(strip_row_count * col_count, samples, strips, chan_piece)
        .transpose(0, 2, 1, 3)
        .reshape(strip_row_count * col_count, chan_count)
    )
    swapped_pool = (
        pooled_wide.reshape(samples, strips, chan_piece).transpose(1, 0, 2).reshape(chan_count)
    )
    tap_terms = (
        lax.dot_general(
            swapped_map, columns_all, (((0,), (0,)), ((), ())), preferred_element_type=jnp.float32
        )
        * factor
    )
    strip_section = lax.psum_scatter(
        jnp.concatenate([tap_terms, swapped_pool[:, None] * image_cols[None, :]], 1).astype(
            jnp.bfloat16
        ),
        STRIP,
        scatter_dimension=0,
        tiled=True,
    )
    shard_part = sum_at_owner(strip_section, SAMPLE, 0)
    weight_total = gather_directly(shard_part.astype(jnp.bfloat16), STRIP, 0).astype(
        shard_part.dtype
    )
    proj_total = total_of_pieces(proj_shard.astype(jnp.bfloat16), STRIP).astype(jnp.float32)
    return (
        result[None],
        input_grad.astype(jnp.bfloat16)[None],
        weight_total[:, :out_width],
        weight_total[:, out_width : 10 * out_width],
        weight_total[:, 10 * out_width :],
        proj_total,
    )


def solution(mesh):
    finer = Mesh(mesh.devices.reshape(8, 2, 4, 4), ("strip_0", "strip_1", "sample_0", "sample_1"))
    placed = (
        P(SAMPLE, STRIP, None, None),
        P(SAMPLE, None),
        P(SAMPLE, None),
        P(SAMPLE, None),
        P(SAMPLE, None),
        P(SAMPLE, STRIP, None, None),
    )
    return jax.shard_map(
        on_device,
        mesh=finer,
        in_specs=placed,
        out_specs=(
            P(SAMPLE, STRIP, None, None),
            P(SAMPLE, STRIP, None, None),
            P(SAMPLE, None),
            P(SAMPLE, None),
            P(SAMPLE, None),
            P(SAMPLE, None),
        ),
        check_vma=False,
    )
```

profile of v0, /device:TPU:1, one launch (start us, length us, event | category | flops | bytes accessed | tf_op | source)
XLA Modules:
  0.0 485.7 jit_solution(9308870175237719834)
XLA Ops:
  7.2 2.1 pad_maximum_fusion.1
  10.3 10.0 %all-to-all-start = ((f32[16,1,2048]{2,1,0:T(1,128)}), f32[16,1,2048]{2,1,0:T(1,128)}, u32[]{:S(2)}, u32[]{:S(2)}) async-start(f32[16,1,2048]{2,1,0:T(1,128)} %broadcast_in_dim.10), calls=%async_computation | async-start | bytes 262144 | tf_op jit(solution)/shard_map/all_to_all | solution.py:29
  20.3 5.3 %collective-permute-start.1 = (bf16[3,108,2048]{2,1,0:T(8,128)(2,1)S(1)}, bf16[3,108,2048]{2,1,0:T(8,128)(2,1)}, u32[]{:S(2)}, u32[]{:S(2)}) collective-permute-start(bf16[3,108,2048]{2,1,0:T(8,128)(2,1)S(1)} %bitcast.155), channel_id=1, source_target_pairs={{0,64},{16,80},{32,96},{48,112},{64,128},{80,144},{96,160},{112,17... | collective-permute-start | bytes 3981320 | tf_op jit(solution)/shard_map/ppermute | solution.py:41
  25.6 1.3 collective-permute-start
  26.9 1.5 copy.26
  28.4 2.6 reshape_reshape_squeeze.3
  31.0 2.8 copy.27
  33.8 20.7 %all_gather.13 = bf16[768,256]{1,0:T(8,128)(2,1)S(1)} all-gather(bf16[48,256]{1,0:T(8,128)(2,1)S(1)} %copy-done.17), channel_id=1, replica_groups=mesh['strip_0'=8,'strip_1'=2,'sample_0'=4,'sample_1'=4] {'sample_0','sam..., dimensions={0}, use_global_device_ids=true | all-gather | bytes 417792 | tf_op jit(solution)/shard_map/all_gather | solution.py:144
  54.5 1.1 reduce_sum.218
  55.9 49.2 %all-gather.3.cloned.1.call-done = bf16[2048,2816]{1,0:T(8,128)(2,1)} async-done(((bf16[128,2816]{1,0:T(8,128)(2,1)}), bf16[2048,2816]{1,0:T(8,128)(2,1)}) %all-gather.3.cloned.1.call-update) | async-done | bytes 11534352 | tf_op jit(solution)/shard_map/all_gather | solution.py:23
  105.1 1.5 fusion.14
  109.2 3.3 fusion.9
  112.5 1.9 copy-done
  114.4 2.6 fusion.7
  117.1 2.6 fusion.8
  120.7 14.3 %all-reduce.11 = (f32[2,256]{1,0:T(2,128)S(1)}, f32[2,256]{1,0:T(2,128)S(1)}) all-reduce(f32[2,256]{1,0:T(2,128)S(1)} %get-tuple-element.88, f32[2,256]{1,0:T(2,128)S(1)} %get-tuple-element.87), channel_id=1, replica_groups=mesh['strip_0'=8,'strip_1'=2,'sample_0'=4,'sample_1'=4] {'strip_0'}, use_global_device_ids=true, to_apply=%region_8.9 | all-reduce | flops 1024 | bytes 8192 | tf_op jit(solution)/shard_map/psum | solution.py:16
  135.0 6.3 %all-reduce.20 = (f32[2,256]{1,0:T(2,128)S(1)}, f32[2,256]{1,0:T(2,128)S(1)}) all-reduce(f32[2,256]{1,0:T(2,128)S(1)} %get-tuple-element.26, f32[2,256]{1,0:T(2,128)S(1)} %get-tuple-element.27), channel_id=1, replica_groups=mesh['strip_0'=8,'strip_1'=2,'sample_0'=4,'sample_1'=4] {'strip_1'}, use_global_device_ids=true, to_apply=%region_9.10 | all-reduce | flops 1024 | bytes 8192 | tf_op jit(solution)/shard_map/psum | solution.py:16
  141.3 8.1 %all-reduce.17 = (f32[2,256]{1,0:T(2,128)S(1)}, f32[2,256]{1,0:T(2,128)S(1)}) all-reduce(f32[2,256]{1,0:T(2,128)S(1)} %get-tuple-element.44, f32[2,256]{1,0:T(2,128)S(1)} %get-tuple-element.45), channel_id=1, replica_groups=mesh['strip_0'=8,'strip_1'=2,'sample_0'=4,'sample_1'=4] {'sample_0'}, use_global_device_ids=true, to_apply=%region_10.11 | all-reduce | flops 1024 | bytes 8192 | tf_op jit(solution)/shard_map/psum | solution.py:16
  149.4 6.5 %all-reduce.14 = (f32[2,256]{1,0:T(2,128)S(1)}, f32[2,256]{1,0:T(2,128)S(1)}) all-reduce(f32[2,256]{1,0:T(2,128)S(1)} %get-tuple-element.38, f32[2,256]{1,0:T(2,128)S(1)} %get-tuple-element.39), channel_id=1, replica_groups=mesh['strip_0'=8,'strip_1'=2,'sample_0'=4,'sample_1'=4] {'sample_1'}, use_global_device_ids=true, to_apply=%region_11.12 | all-reduce | flops 1024 | bytes 8192 | tf_op jit(solution)/shard_map/psum | solution.py:16
  156.6 11.5 %all-reduce.10 = (f32[1,256]{1,0:T(1,128)S(1)}, f32[1,256]{1,0:T(1,128)S(1)}) all-reduce(f32[1,256]{1,0:T(1,128)S(1)} %bitcast.198, f32[1,256]{1,0:T(1,128)S(1)} %bitcast.197), channel_id=1, replica_groups=mesh['strip_0'=8,'strip_1'=2,'sample_0'=4,'sample_1'=4] {'strip_0'}, use_global_device_ids=true, to_apply=%region_22.23 | all-reduce | flops 512 | bytes 4096 | tf_op jit(solution)/shard_map/psum | solution.py:16
  168.2 10.2 %all-reduce.19 = (f32[1,256]{1,0:T(1,128)S(1)}, f32[1,256]{1,0:T(1,128)S(1)}) all-reduce(f32[1,256]{1,0:T(1,128)S(1)} %get-tuple-element.24, f32[1,256]{1,0:T(1,128)S(1)} %get-tuple-element.25), channel_id=1, replica_groups=mesh['strip_0'=8,'strip_1'=2,'sample_0'=4,'sample_1'=4] {'strip_1'}, use_global_device_ids=true, to_apply=%region_23.24 | all-reduce | flops 512 | bytes 4096 | tf_op jit(solution)/shard_map/psum | solution.py:16
  178.4 6.8 %all-reduce.16 = (f32[1,256]{1,0:T(1,128)S(1)}, f32[1,256]{1,0:T(1,128)S(1)}) all-reduce(f32[1,256]{1,0:T(1,128)S(1)} %get-tuple-element.42, f32[1,256]{1,0:T(1,128)S(1)} %get-tuple-element.43), channel_id=1, replica_groups=mesh['strip_0'=8,'strip_1'=2,'sample_0'=4,'sample_1'=4] {'sample_0'}, use_global_device_ids=true, to_apply=%region_24.25 | all-reduce | flops 512 | bytes 4096 | tf_op jit(solution)/shard_map/psum | solution.py:16
  185.2 6.1 %all-reduce.13 = (f32[1,256]{1,0:T(1,128)S(1)}, f32[1,256]{1,0:T(1,128)S(1)}) all-reduce(f32[1,256]{1,0:T(1,128)S(1)} %get-tuple-element.36, f32[1,256]{1,0:T(1,128)S(1)} %get-tuple-element.37), channel_id=1, replica_groups=mesh['strip_0'=8,'strip_1'=2,'sample_0'=4,'sample_1'=4] {'sample_1'}, use_global_device_ids=true, to_apply=%region_25.26 | all-reduce | flops 512 | bytes 4096 | tf_op jit(solution)/shard_map/psum | solution.py:16
  191.6 11.4 %all-reduce.9 = (f32[256]{0:T(256)S(1)}, f32[256]{0:T(256)S(1)}) all-reduce(f32[256]{0:T(256)S(1)} %get-tuple-element.13, f32[256]{0:T(256)S(1)} %get-tuple-element.12), channel_id=1, replica_groups=mesh['strip_0'=8,'strip_1'=2,'sample_0'=4,'sample_1'=4] {'strip_0'}, use_global_device_ids=true, to_apply=%region_32.33 | all-reduce | flops 512 | bytes 4096 | tf_op jit(solution)/shard_map/psum | solution.py:16
  202.9 9.8 %all-reduce.18 = (f32[256]{0:T(256)S(1)}, f32[256]{0:T(256)S(1)}) all-reduce(f32[256]{0:T(256)S(1)} %get-tuple-element.22, f32[256]{0:T(256)S(1)} %get-tuple-element.23), channel_id=1, replica_groups=mesh['strip_0'=8,'strip_1'=2,'sample_0'=4,'sample_1'=4] {'strip_1'}, use_global_device_ids=true, to_apply=%region_33.34 | all-reduce | flops 512 | bytes 4096 | tf_op jit(solution)/shard_map/psum | solution.py:16
  212.7 7.7 %all-reduce.15 = (f32[256]{0:T(256)S(1)}, f32[256]{0:T(256)S(1)}) all-reduce(f32[256]{0:T(256)S(1)} %get-tuple-element.40, f32[256]{0:T(256)S(1)} %get-tuple-element.41), channel_id=1, replica_groups=mesh['strip_0'=8,'strip_1'=2,'sample_0'=4,'sample_1'=4] {'sample_0'}, use_global_device_ids=true, to_apply=%region_34.35 | all-reduce | flops 512 | bytes 4096 | tf_op jit(solution)/shard_map/psum | solution.py:16
  220.4 6.5 %all-reduce.12 = (f32[256]{0:T(256)S(1)}, f32[256]{0:T(256)S(1)}) all-reduce(f32[256]{0:T(256)S(1)} %get-tuple-element.34, f32[256]{0:T(256)S(1)} %get-tuple-element.35), channel_id=1, replica_groups=mesh['strip_0'=8,'strip_1'=2,'sample_0'=4,'sample_1'=4] {'sample_1'}, use_global_device_ids=true, to_apply=%region_35.36 | all-reduce | flops 512 | bytes 4096 | tf_op jit(solution)/shard_map/psum | solution.py:16
  227.0 0.9 fusion.74
  228.5 11.5 %psum.220 = f32[4,256]{1,0:T(4,128)S(1)} all-reduce(f32[4,256]{1,0:T(4,128)S(1)} %pad_maximum_fusion.6), channel_id=1, replica_groups=mesh['strip_0'=8,'strip_1'=2,'sample_0'=4,'sample_1'=4] {'strip_0'}, use_global_device_ids=true, to_apply=%region_40.41 | all-reduce | flops 1024 | bytes 8192 | tf_op jit(solution)/shard_map/psum | solution.py:16
  240.0 10.3 %psum.221 = f32[4,256]{1,0:T(4,128)S(1)} all-reduce(f32[4,256]{1,0:T(4,128)S(1)} %psum.220), channel_id=1, replica_groups=mesh['strip_0'=8,'strip_1'=2,'sample_0'=4,'sample_1'=4] {'strip_1'}, use_global_device_ids=true, to_apply=%region_41.42 | all-reduce | flops 1024 | bytes 8192 | tf_op jit(solution)/shard_map/psum | solution.py:16
  250.3 6.8 %psum.222 = f32[4,256]{1,0:T(4,128)S(1)} all-reduce(f32[4,256]{1,0:T(4,128)S(1)} %psum.221), channel_id=1, replica_groups=mesh['strip_0'=8,'strip_1'=2,'sample_0'=4,'sample_1'=4] {'sample_0'}, use_global_device_ids=true, to_apply=%region_42.43 | all-reduce | flops 1024 | bytes 8192 | tf_op jit(solution)/shard_map/psum | solution.py:16
  257.1 6.1 %psum.223 = f32[4,256]{1,0:T(4,128)S(1)} all-reduce(f32[4,256]{1,0:T(4,128)S(1)} %psum.222), channel_id=1, replica_groups=mesh['strip_0'=8,'strip_1'=2,'sample_0'=4,'sample_1'=4] {'sample_1'}, use_global_device_ids=true, to_apply=%region_43.44 | all-reduce | flops 1024 | bytes 8192 | tf_op jit(solution)/shard_map/psum | solution.py:16
  263.5 1.9 collective-permute-start.3
  265.4 1.3 collective-permute-start.2
  267.3 13.6 %all-to-all-start.1 = ((f32[16,1,256]{2,1,0:T(1,128)}), f32[16,1,256]{2,1,0:T(1,128)S(1)}, u32[]{:S(2)}, u32[]{:S(2)}) async-start(f32[16,1,256]{2,1,0:T(1,128)} %broadcast_in_dim.12), calls=%async_computation.1 | async-start | bytes 32768 | tf_op jit(solution)/shard_map/all_to_all | solution.py:29
  281.2 0.9 constant_dynamic-update-slice_fusion.9
  282.1 6.2 %all-to-all-done.1 = f32[16,1,256]{2,1,0:T(1,128)S(1)} async-done(((f32[16,1,256]{2,1,0:T(1,128)}), f32[16,1,256]{2,1,0:T(1,128)S(1)}, u32[]{:S(2)}, u32[]{:S(2)}) %all-to-all-start.1) | async-done | bytes 16416 | tf_op jit(solution)/shard_map/all_to_all | solution.py:29
  288.3 1.0 fusion.52
  293.0 0.8 constant_dynamic-update-slice_fusion.6
  295.3 0.9 constant_dynamic-update-slice_fusion.3
  296.1 0.8 constant_dynamic-update-slice_fusion.2
  297.6 0.9 constant_dynamic-update-slice_fusion
  298.4 2.7 reshape.81
  301.1 7.6 %fusion = bf16[2048,2560]{0,1:T(8,128)(2,1)S(1)} fusion(bf16[324,2560]{1,0:T(8,128)(2,1)} %reshape.81, bf16[324,2048]{0,1:T(8,128)(2,1)} %bitcast.157), kind=kOutput, calls=%fused_computation.2 | convolution fusion | flops 3407872000 | bytes 13471744 | tf_op jit(solution)/shard_map/dot_general | solution.py:258
  308.8 11.3 %pad_maximum_fusion = bf16[2048,2816]{0,1:T(8,128)(2,1)} fusion(bf16[2048,256]{0,1:T(8,128)(2,1)S(1)} %multiply_convert_fusion.1, bf16[2048,2560]{0,1:T(8,128)(2,1)S(1)} %fusion), kind=kLoop, calls=%fused_computation.1 | loop fusion | flops 23068672 | bytes 23068672 | tf_op jit(solution)/shard_map/concatenate | solution.py:264
  320.1 15.3 %copy.30 = bf16[2048,2816]{1,0:T(8,128)(2,1)} copy(bf16[2048,2816]{0,1:T(8,128)(2,1)} %pad_maximum_fusion) | data formatting | bytes 23068672
  335.7 67.2 %reduce-scatter.4.cloned.1.call-done = bf16[128,2816]{1,0:T(8,128)(2,1)} async-done(((bf16[2048,2816]{1,0:T(8,128)(2,1)}), bf16[128,2816]{1,0:T(8,128)(2,1)}) %reduce-scatter.4.cloned.1.call-update) | async-done | bytes 720912 | tf_op jit(solution)/shard_map/reduce_scatter | solution.py:263
  403.0 6.4 %all-to-all-start.2 = ((bf16[16,8,2816]{2,1,0:T(8,128)(2,1)}), bf16[16,8,2816]{2,1,0:T(8,128)(2,1)S(1)}, u32[]{:S(2)}, u32[]{:S(2)}) async-start(bf16[16,8,2816]{2,1,0:T(8,128)(2,1)} %bitcast.159), calls=%async_computation.2 | async-start | bytes 1441792 | tf_op jit(solution)/shard_map/all_to_all | solution.py:51
  409.5 0.8 pad_maximum_fusion.2
  410.3 1.6 fusion.12
  411.9 7.8 %all-to-all-done.2 = bf16[16,8,2816]{2,1,0:T(8,128)(2,1)S(1)} async-done(((bf16[16,8,2816]{2,1,0:T(8,128)(2,1)}), bf16[16,8,2816]{2,1,0:T(8,128)(2,1)S(1)}, u32[]{:S(2)}, u32[]{:S(2)}) %all-to-all-start.2) | async-done | bytes 720928 | tf_op jit(solution)/shard_map/all_to_all | solution.py:51
  419.7 4.2 all-to-all-start.4
  423.9 2.0 convolution_add_fusion
  426.0 1.3 reduce_sum.233
  427.2 4.9 %all-to-all-done.4 = bf16[16,48,256]{2,1,0:T(8,128)(2,1)} async-done(((bf16[16,48,256]{2,1,0:T(8,128)(2,1)}), bf16[16,48,256]{2,1,0:T(8,128)(2,1)}, u32[]{:S(2)}, u32[]{:S(2)}) %all-to-all-start.4) | async-done | bytes 393248 | tf_op jit(solution)/shard_map/all_to_all | solution.py:51
  432.2 0.9 broadcast_in_dim.14
  433.1 11.1 %all-to-all-start.3 = ((bf16[16,8,2816]{2,1,0:T(8,128)(2,1)}), bf16[16,8,2816]{2,1,0:T(8,128)(2,1)}, u32[]{:S(2)}, u32[]{:S(2)}) async-start(bf16[16,8,2816]{2,1,0:T(8,128)(2,1)} %broadcast_in_dim.14), calls=%async_computation.3 | async-start | bytes 1441792 | tf_op jit(solution)/shard_map/all_to_all | solution.py:29
  444.2 3.3 fusion.3
  447.6 3.2 convolution_add_fusion.2
  450.8 4.3 fusion.2
  455.1 1.1 reduce_sum.234
  456.2 19.0 %all-gather = bf16[768,256]{1,0:T(8,128)(2,1)S(1)} all-gather(bf16[48,256]{1,0:T(8,128)(2,1)S(1)} %reduce_sum.234), channel_id=2, replica_groups=mesh['strip_0'=8,'strip_1'=2,'sample_0'=4,'sample_1'=4] {'strip_0','stri..., dimensions={0}, use_global_device_ids=true | all-gather | bytes 417792 | tf_op jit(solution)/shard_map/all_gather | solution.py:67
  475.9 1.2 bitcast_convert_fusion
  477.8 1.1 slice.191
  (97 shorter events, 12.4 us)
Async XLA Ops:
  7.2 2.2 copy-start.1
  7.2 97.9 %all-gather.3.cloned.1.call-start = ((), (), s32[]{:S(2)}) async-start(), calls=%async_computation.6 | async-start | bytes 12255232 | tf_op jit(solution)/shard_map/all_gather | solution.py:23
  10.3 44.2 %all-to-all-start = ((f32[16,1,2048]{2,1,0:T(1,128)}), f32[16,1,2048]{2,1,0:T(1,128)}, u32[]{:S(2)}, u32[]{:S(2)}) async-start(f32[16,1,2048]{2,1,0:T(1,128)} %broadcast_in_dim.10), calls=%async_computation | async-start | bytes 262144 | tf_op jit(solution)/shard_map/all_to_all | solution.py:29
  20.3 92.2 %collective-permute-start.1 = (bf16[3,108,2048]{2,1,0:T(8,128)(2,1)S(1)}, bf16[3,108,2048]{2,1,0:T(8,128)(2,1)}, u32[]{:S(2)}, u32[]{:S(2)}) collective-permute-start(bf16[3,108,2048]{2,1,0:T(8,128)(2,1)S(1)} %bitcast.155), channel_id=1, source_target_pairs={{0,64},{16,80},{32,96},{48,112},{64,128},{80,144},{96,160},{112,17... | collective-permute-start | bytes 3981320 | tf_op jit(solution)/shard_map/ppermute | solution.py:41
  25.6 91.5 %collective-permute-start = (bf16[3,108,2048]{2,1,0:T(8,128)(2,1)S(1)}, bf16[3,108,2048]{2,1,0:T(8,128)(2,1)}, u32[]{:S(2)}, u32[]{:S(2)}) collective-permute-start(bf16[3,108,2048]{2,1,0:T(8,128)(2,1)S(1)} %bitcast.156), channel_id=1, source_target_pairs={{64,0},{80,16},{96,32},{112,48},{128,64},{144,80},{160,96},{176,11... | collective-permute-start | bytes 3981320 | tf_op jit(solution)/shard_map/ppermute | solution.py:41
  31.0 2.8 copy-start.17
  54.5 173.4 %copy-start.10 = (bf16[768,256]{1,0:T(8,128)(2,1)}, bf16[768,256]{1,0:T(8,128)(2,1)S(1)}, u32[]{:S(2)}) copy-start(bf16[768,256]{1,0:T(8,128)(2,1)S(1)} %all_gather.13) | copy-start | bytes 1179652
  109.2 5.2 %copy-start = (bf16[2048,2816]{1,0:T(8,128)(2,1)S(1)}, bf16[2048,2816]{1,0:T(8,128)(2,1)}, u32[]{:S(2)}) copy-start(bf16[2048,2816]{1,0:T(8,128)(2,1)} %all-gather.3.cloned.1.call-done) | copy-start | bytes 34603012
  120.6 170.7 %copy-start.2 = (f32[256,3,108]{0,2,1:T(8,128)}, f32[256,3,108]{0,2,1:T(8,128)S(1)}, u32[]{:S(2)}) copy-start(f32[256,3,108]{0,2,1:T(8,128)S(1)} %get-tuple-element.85) | copy-start | bytes 995332
  120.6 70.7 %copy-start.13 = (bf16[1,3,108,256]{3,2,1,0:T(8,128)(2,1)S(1)}, bf16[1,3,108,256]{3,2,1,0:T(8,128)(2,1)}, u32[]{:S(2)}) copy-start(bf16[1,3,108,256]{3,2,1,0:T(8,128)(2,1)} %param.11) | copy-start | bytes 497668
  263.5 31.8 %copy-start.6 = (bf16[3,108,256]{2,1,0:T(8,128)(2,1)}, bf16[3,108,256]{2,1,0:T(8,128)(2,1)S(1)}, u32[]{:S(2)}) copy-start(bf16[3,108,256]{2,1,0:T(8,128)(2,1)S(1)} %multiply_convert_fusion.2) | copy-start | bytes 497668
  263.5 32.7 %collective-permute-start.3 = (bf16[3,108,256]{2,1,0:T(8,128)(2,1)S(1)}, bf16[3,108,256]{2,1,0:T(8,128)(2,1)S(1)}, u32[]{:S(2)}, u32[]{:S(2)}) collective-permute-start(bf16[3,108,256]{2,1,0:T(8,128)(2,1)S(1)} %multiply_convert_fusion.2), channel_id=1, source_target_pairs={{0,64},{16,80},{32,96},{48,112},{64,128},{80,144},{96,160},{112,17... | collective-permute-start | bytes 497672 | tf_op jit(solution)/shard_map/ppermute | solution.py:41
  265.4 26.2 %collective-permute-start.2 = (bf16[3,108,256]{2,1,0:T(8,128)(2,1)S(1)}, bf16[3,108,256]{2,1,0:T(8,128)(2,1)S(1)}, u32[]{:S(2)}, u32[]{:S(2)}) collective-permute-start(bf16[3,108,256]{2,1,0:T(8,128)(2,1)S(1)} %multiply_convert_fusion.2), channel_id=1, source_target_pairs={{64,0},{80,16},{96,32},{112,48},{128,64},{144,80},{160,96},{176,11... | collective-permute-start | bytes 497672 | tf_op jit(solution)/shard_map/ppermute | solution.py:41
  267.3 21.0 %all-to-all-start.1 = ((f32[16,1,256]{2,1,0:T(1,128)}), f32[16,1,256]{2,1,0:T(1,128)S(1)}, u32[]{:S(2)}, u32[]{:S(2)}) async-start(f32[16,1,256]{2,1,0:T(1,128)} %broadcast_in_dim.12), calls=%async_computation.1 | async-start | bytes 32768 | tf_op jit(solution)/shard_map/all_to_all | solution.py:29
  280.9 122.0 %reduce-scatter.4.cloned.1.call-start = ((), (), s32[]{:S(2)}) async-start(), calls=%async_computation.7 | async-start | bytes 12255232 | tf_op jit(solution)/shard_map/reduce_scatter | solution.py:263
  291.5 9.6 %copy-start.4 = (bf16[3,108,256]{2,1,0:T(8,128)(2,1)}, bf16[3,108,256]{2,1,0:T(8,128)(2,1)S(1)}, u32[]{:S(2)}) copy-start(bf16[3,108,256]{2,1,0:T(8,128)(2,1)S(1)} %collective-permute-done.2) | copy-start | bytes 497668
  296.1 5.0 %copy-start.8 = (bf16[3,108,256]{2,1,0:T(8,128)(2,1)}, bf16[3,108,256]{2,1,0:T(8,128)(2,1)S(1)}, u32[]{:S(2)}) copy-start(bf16[3,108,256]{2,1,0:T(8,128)(2,1)S(1)} %collective-permute-done.3) | copy-start | bytes 497668
  403.0 16.8 %all-to-all-start.2 = ((bf16[16,8,2816]{2,1,0:T(8,128)(2,1)}), bf16[16,8,2816]{2,1,0:T(8,128)(2,1)S(1)}, u32[]{:S(2)}, u32[]{:S(2)}) async-start(bf16[16,8,2816]{2,1,0:T(8,128)(2,1)} %bitcast.159), calls=%async_computation.2 | async-start | bytes 1441792 | tf_op jit(solution)/shard_map/all_to_all | solution.py:51
  419.7 4.2 copy-start.3
  419.7 12.5 %all-to-all-start.4 = ((bf16[16,48,256]{2,1,0:T(8,128)(2,1)}), bf16[16,48,256]{2,1,0:T(8,128)(2,1)}, u32[]{:S(2)}, u32[]{:S(2)}) async-start(bf16[16,48,256]{2,1,0:T(8,128)(2,1)} %bitcast.45), calls=%async_computation.4 | async-start | bytes 786432 | tf_op jit(solution)/shard_map/all_to_all | solution.py:51
  426.0 18.2 %copy-start.7 = (bf16[3,108,256]{2,1,0:T(8,128)(2,1)S(1)}, bf16[3,108,256]{2,1,0:T(8,128)(2,1)}, u32[]{:S(2)}) copy-start(bf16[3,108,256]{2,1,0:T(8,128)(2,1)} %copy-done.6) | copy-start | bytes 497668
  426.0 18.2 %copy-start.16 = (bf16[3,108,256]{2,1,0:T(8,128)(2,1)S(1)}, bf16[3,108,256]{2,1,0:T(8,128)(2,1)}, u32[]{:S(2)}) copy-start(bf16[3,108,256]{2,1,0:T(8,128)(2,1)} %get-tuple-element.68) | copy-start | bytes 497668
  433.1 42.8 %all-to-all-start.3 = ((bf16[16,8,2816]{2,1,0:T(8,128)(2,1)}), bf16[16,8,2816]{2,1,0:T(8,128)(2,1)}, u32[]{:S(2)}, u32[]{:S(2)}) async-start(bf16[16,8,2816]{2,1,0:T(8,128)(2,1)} %broadcast_in_dim.14), calls=%async_computation.3 | async-start | bytes 1441792 | tf_op jit(solution)/shard_map/all_to_all | solution.py:29
  444.2 3.3 copy-start.5
  444.2 3.3 copy-start.11
  444.2 3.3 copy-start.12
  447.5 3.3 copy-start.9
  447.6 3.3 copy-start.14
  447.6 3.3 copy-start.15
Sparse Core Ops, SparseCore 0:
  11.0 94.0 all-gather.2
  335.5 67.3 reduce-scatter.3
where the time goes:
time: 487 us; the launch traced here: 486 us
  blocking collectives  180 us (37%)
  waiting for transfers between devices  135 us (28%)
  starting transfers between devices  55.3 us (11%)
  local copies, waits for them, and re-layouts  38.2 us (8%)
  matrix products  34.6 us (7%)
  other arithmetic  25.1 us (5%)
  between operations  17.3 us (4%)
    psum x16, blocking collectives, one_axis_at_a_time(): array = lax.psum(array, axis)  140 us
    reduce_scatter x1, waiting for transfers between devices, on_device(): lax.psum_scatter(jnp.concatenate([tap_terms, swapped_pool[:, None] * imag...  67.2 us
    all_gather x1, waiting for transfers between devices, side_by_side(): filled = lax.all_gather(both, axis, axis=dim, tiled=True)  49.2 us
    all_to_all x3, starting transfers between devices, from_everyone(): lax.all_to_all(jnp.broadcast_to(array[None], (peers, *array.shape)), axis...  34.7 us
    unnamed x46, local copies, waits for them, and re-layouts  24.8 us
    all_gather x1, blocking collectives, on_device(): lax.all_gather(w_proj, SAMPLE, axis=0, tiled=True)  20.7 us
    all_gather x1, blocking collectives, total_of_pieces(): return lax.all_gather(array, axis).astype(jnp.float32).sum(0)  19 us
    dot_general x7, matrix products, contract_last(): lax.dot_general(left, right, (((left.ndim - 1,), (1,)), ((), ())), prefer...  15.7 us
  transfers between devices with their start and end apart: 11, of which 5 were waited for; matrix products, arithmetic and copies ran while one was open for 9% of the time, Pallas kernels for 0%

commit v1 on v0

--- a/solution.py
+++ b/solution.py
@@ -13,7 +13,7 @@
 
 def one_axis_at_a_time(array, axes):
     for axis in axes:
-        array = lax.psum(array, axis)
+        array = jnp.sum(lax.all_gather(array, axis), axis=0)
     return array
 
 

time: 487 us -> 613 us (1.26)
  blocking collectives: 180 us -> 304 us
    all_gather x0 -> x28, blocking collectives: none -> 264 us  [one_axis_at_a_time(): array = jnp.sum(lax.all_gather(array, axis), axis=0)]
    psum x16 -> x0, blocking collectives: 140 us -> none  [one_axis_at_a_time(): array = lax.psum(array, axis)]
  transfers between devices with their start and end apart: 11 -> 11, of which waited for: 5 -> 5; matrix products, arithmetic and copies ran while one was open for 9% -> 7% of each run, Pallas kernels for 0% -> 0%
where the time goes in v1:
time: 613 us; the launch traced here: 612 us
  blocking collectives  304 us (50%)
  waiting for transfers between devices  136 us (22%)
  starting transfers between devices  56.4 us (9%)
  local copies, waits for them, and re-layouts  38.2 us (6%)
  matrix products  34.6 us (6%)
  other arithmetic  25.7 us (4%)
  between operations  17.3 us (3%)
    all_gather x28, blocking collectives, one_axis_at_a_time(): array = jnp.sum(lax.all_gather(array, axis), axis=0)  264 us
    reduce_scatter x1, waiting for transfers between devices, on_device(): lax.psum_scatter(jnp.concatenate([tap_terms, swapped_pool[:, None] * imag...  67.4 us
    all_gather x1, waiting for transfers between devices, side_by_side(): filled = lax.all_gather(both, axis, axis=dim, tiled=True)  49.2 us
    all_to_all x3, starting transfers between devices, from_everyone(): lax.all_to_all(jnp.broadcast_to(array[None], (peers, *array.shape)), axis...  35.1 us
    unnamed x46, local copies, waits for them, and re-layouts  24.8 us
    all_gather x1, blocking collectives, on_device(): lax.all_gather(w_proj, SAMPLE, axis=0, tiled=True)  20.7 us
    all_gather x1, blocking collectives, total_of_pieces(): return lax.all_gather(array, axis).astype(jnp.float32).sum(0)  19 us
    dot_general x7, matrix products, contract_last(): lax.dot_general(left, right, (((left.ndim - 1,), (1,)), ((), ())), prefer...  15.7 us
  transfers between devices with their start and end apart: 11, of which 5 were waited for; matrix products, arithmetic and copies ran while one was open for 7% of the time, Pallas kernels for 0%

profile of v1, /device:TPU:1, one launch (start us, length us, event | category | flops | bytes accessed | tf_op | source)
XLA Modules:
  0.0 611.6 jit_solution(15487878968915683979)
XLA Ops:
  7.2 2.1 pad_maximum_fusion.1
  10.3 10.0 %all-to-all-start = ((f32[16,1,2048]{2,1,0:T(1,128)}), f32[16,1,2048]{2,1,0:T(1,128)}, u32[]{:S(2)}, u32[]{:S(2)}) async-start(f32[16,1,2048]{2,1,0:T(1,128)} %broadcast_in_dim.10), calls=%async_computation | async-start | bytes 262144 | tf_op jit(solution)/shard_map/all_to_all | solution.py:29
  20.3 5.3 collective-permute-start.1
  25.6 1.3 collective-permute-start
  26.9 1.5 copy.26
  28.4 2.6 reshape_reshape_squeeze.3
  31.0 2.8 copy.27
  33.8 20.7 %all_gather.191 = bf16[768,256]{1,0:T(8,128)(2,1)S(1)} all-gather(bf16[48,256]{1,0:T(8,128)(2,1)S(1)} %copy-done.17), channel_id=1, replica_groups=mesh['strip_0'=8,'strip_1'=2,'sample_0'=4,'sample_1'=4] {'sample_0','sam..., dimensions={0}, use_global_device_ids=true | all-gather | bytes 417792 | tf_op jit(solution)/shard_map/all_gather | solution.py:144
  55.9 49.2 %all-gather.59.cloned.1.call-done = bf16[2048,2816]{1,0:T(8,128)(2,1)} async-done(((bf16[128,2816]{1,0:T(8,128)(2,1)}), bf16[2048,2816]{1,0:T(8,128)(2,1)}) %all-gather.59.cloned.1.call-update) | async-done | bytes 11534352 | tf_op jit(solution)/shard_map/all_gather | solution.py:23
  105.1 1.5 fusion.14
  109.2 3.3 fusion.9
  112.5 1.9 copy-done
  114.4 2.6 fusion.7
  117.1 2.6 fusion.8
  120.7 18.6 %all-gather.33 = f32[8,2,256]{2,1,0:T(2,128)S(1)} all-gather(f32[1,2,256]{2,1,0:T(2,128)S(1)} %maximum_bitcast_fusion.2), channel_id=6, replica_groups=mesh['strip_0'=8,'strip_1'=2,'sample_0'=4,'sample_1'=4] {'strip_0'}, dimensions={0}, use_global_device_ids=true | all-gather | bytes 18432 | tf_op jit(solution)/shard_map/all_gather | solution.py:16
  139.3 7.9 %all-gather.34 = f32[2,2,256]{2,1,0:T(2,128)S(1)} all-gather(f32[1,2,256]{2,1,0:T(2,128)S(1)} %bitcast.209), channel_id=7, replica_groups=mesh['strip_0'=8,'strip_1'=2,'sample_0'=4,'sample_1'=4] {'strip_1'}, dimensions={0}, use_global_device_ids=true | all-gather | bytes 6144 | tf_op jit(solution)/shard_map/all_gather | solution.py:16
  147.2 8.3 %all-gather.35 = f32[4,2,256]{2,1,0:T(2,128)S(1)} all-gather(f32[1,2,256]{2,1,0:T(2,128)S(1)} %bitcast.211), channel_id=8, replica_groups=mesh['strip_0'=8,'strip_1'=2,'sample_0'=4,'sample_1'=4] {'sample_0'}, dimensions={0}, use_global_device_ids=true | all-gather | bytes 10240 | tf_op jit(solution)/shard_map/all_gather | solution.py:16
  155.5 8.1 %all-gather.36 = f32[4,2,256]{2,1,0:T(2,128)S(1)} all-gather(f32[1,2,256]{2,1,0:T(2,128)S(1)} %bitcast.213), channel_id=9, replica_groups=mesh['strip_0'=8,'strip_1'=2,'sample_0'=4,'sample_1'=4] {'sample_1'}, dimensions={0}, use_global_device_ids=true | all-gather | bytes 10240 | tf_op jit(solution)/shard_map/all_gather | solution.py:16
  163.7 15.5 %all-gather.29 = f32[8,2,256]{2,1,0:T(2,128)S(1)} all-gather(f32[1,2,256]{2,1,0:T(2,128)S(1)} %maximum_bitcast_fusion.1), channel_id=2, replica_groups=mesh['strip_0'=8,'strip_1'=2,'sample_0'=4,'sample_1'=4] {'strip_0'}, dimensions={0}, use_global_device_ids=true | all-gather | bytes 18432 | tf_op jit(solution)/shard_map/all_gather | solution.py:16
  179.1 12.4 %all-gather.30 = f32[2,2,256]{2,1,0:T(2,128)S(1)} all-gather(f32[1,2,256]{2,1,0:T(2,128)S(1)} %bitcast.210), channel_id=3, replica_groups=mesh['strip_0'=8,'strip_1'=2,'sample_0'=4,'sample_1'=4] {'strip_1'}, dimensions={0}, use_global_device_ids=true | all-gather | bytes 6144 | tf_op jit(solution)/shard_map/all_gather | solution.py:16
  191.5 8.1 %all-gather.31 = f32[4,2,256]{2,1,0:T(2,128)S(1)} all-gather(f32[1,2,256]{2,1,0:T(2,128)S(1)} %bitcast.212), channel_id=4, replica_groups=mesh['strip_0'=8,'strip_1'=2,'sample_0'=4,'sample_1'=4] {'sample_0'}, dimensions={0}, use_global_device_ids=true | all-gather | bytes 10240 | tf_op jit(solution)/shard_map/all_gather | solution.py:16
  199.6 8.1 %all-gather.32 = f32[4,2,256]{2,1,0:T(2,128)S(1)} all-gather(f32[1,2,256]{2,1,0:T(2,128)S(1)} %bitcast.214), channel_id=5, replica_groups=mesh['strip_0'=8,'strip_1'=2,'sample_0'=4,'sample_1'=4] {'sample_1'}, dimensions={0}, use_global_device_ids=true | all-gather | bytes 10240 | tf_op jit(solution)/shard_map/all_gather | solution.py:16
  208.4 10.0 %all-gather.41 = f32[8,1,256]{2,1,0:T(1,128)S(1)} all-gather(f32[1,1,256]{2,1,0:T(1,128)S(1)} %bitcast.244), channel_id=14, replica_groups=mesh['strip_0'=8,'strip_1'=2,'sample_0'=4,'sample_1'=4] {'strip_0'}, dimensions={0}, use_global_device_ids=true | all-gather | bytes 9216 | tf_op jit(solution)/shard_map/all_gather | solution.py:16
  218.4 9.7 %all-gather.42 = f32[2,1,256]{2,1,0:T(1,128)S(1)} all-gather(f32[1,1,256]{2,1,0:T(1,128)S(1)} %bitcast.226), channel_id=15, replica_groups=mesh['strip_0'=8,'strip_1'=2,'sample_0'=4,'sample_1'=4] {'strip_1'}, dimensions={0}, use_global_device_ids=true | all-gather | bytes 3072 | tf_op jit(solution)/shard_map/all_gather | solution.py:16
  228.2 6.5 %all-gather.43 = f32[4,1,256]{2,1,0:T(1,128)S(1)} all-gather(f32[1,1,256]{2,1,0:T(1,128)S(1)} %bitcast.227), channel_id=16, replica_groups=mesh['strip_0'=8,'strip_1'=2,'sample_0'=4,'sample_1'=4] {'sample_0'}, dimensions={0}, use_global_device_ids=true | all-gather | bytes 5120 | tf_op jit(solution)/shard_map/all_gather | solution.py:16
  234.7 5.3 all-gather.44
  240.0 11.5 %all-gather.37 = f32[8,1,256]{2,1,0:T(1,128)S(1)} all-gather(f32[1,1,256]{2,1,0:T(1,128)S(1)} %bitcast.243), channel_id=10, replica_groups=mesh['strip_0'=8,'strip_1'=2,'sample_0'=4,'sample_1'=4] {'strip_0'}, dimensions={0}, use_global_device_ids=true | all-gather | bytes 9216 | tf_op jit(solution)/shard_map/all_gather | solution.py:16
  251.6 9.4 %all-gather.38 = f32[2,1,256]{2,1,0:T(1,128)S(1)} all-gather(f32[1,1,256]{2,1,0:T(1,128)S(1)} %bitcast.228), channel_id=11, replica_groups=mesh['strip_0'=8,'strip_1'=2,'sample_0'=4,'sample_1'=4] {'strip_1'}, dimensions={0}, use_global_device_ids=true | all-gather | bytes 3072 | tf_op jit(solution)/shard_map/all_gather | solution.py:16
  261.0 6.7 %all-gather.39 = f32[4,1,256]{2,1,0:T(1,128)S(1)} all-gather(f32[1,1,256]{2,1,0:T(1,128)S(1)} %bitcast.229), channel_id=12, replica_groups=mesh['strip_0'=8,'strip_1'=2,'sample_0'=4,'sample_1'=4] {'sample_0'}, dimensions={0}, use_global_device_ids=true | all-gather | bytes 5120 | tf_op jit(solution)/shard_map/all_gather | solution.py:16
  267.7 5.5 all-gather.40
  273.5 10.1 %all-gather.49 = f32[8,1,256]{2,1,0:T(1,128)S(1)} all-gather(f32[1,1,256]{2,1,0:T(1,128)S(1)} %bitcast.216), channel_id=22, replica_groups=mesh['strip_0'=8,'strip_1'=2,'sample_0'=4,'sample_1'=4] {'strip_0'}, dimensions={0}, use_global_device_ids=true | all-gather | bytes 9216 | tf_op jit(solution)/shard_map/all_gather | solution.py:16
  283.6 9.0 %all-gather.50 = f32[2,1,256]{2,1,0:T(1,128)S(1)} all-gather(f32[1,1,256]{2,1,0:T(1,128)S(1)} %bitcast.230), channel_id=23, replica_groups=mesh['strip_0'=8,'strip_1'=2,'sample_0'=4,'sample_1'=4] {'strip_1'}, dimensions={0}, use_global_device_ids=true | all-gather | bytes 3072 | tf_op jit(solution)/shard_map/all_gather | solution.py:16
  292.6 6.5 %all-gather.51 = f32[4,1,256]{2,1,0:T(1,128)S(1)} all-gather(f32[1,1,256]{2,1,0:T(1,128)S(1)} %bitcast.231), channel_id=24, replica_groups=mesh['strip_0'=8,'strip_1'=2,'sample_0'=4,'sample_1'=4] {'sample_0'}, dimensions={0}, use_global_device_ids=true | all-gather | bytes 5120 | tf_op jit(solution)/shard_map/all_gather | solution.py:16
  299.1 5.3 all-gather.52
  304.5 11.5 %all-gather.45 = f32[8,1,256]{2,1,0:T(1,128)S(1)} all-gather(f32[1,1,256]{2,1,0:T(1,128)S(1)} %bitcast.215), channel_id=18, replica_groups=mesh['strip_0'=8,'strip_1'=2,'sample_0'=4,'sample_1'=4] {'strip_0'}, dimensions={0}, use_global_device_ids=true | all-gather | bytes 9216 | tf_op jit(solution)/shard_map/all_gather | solution.py:16
  316.1 9.4 %all-gather.46 = f32[2,1,256]{2,1,0:T(1,128)S(1)} all-gather(f32[1,1,256]{2,1,0:T(1,128)S(1)} %bitcast.232), channel_id=19, replica_groups=mesh['strip_0'=8,'strip_1'=2,'sample_0'=4,'sample_1'=4] {'strip_1'}, dimensions={0}, use_global_device_ids=true | all-gather | bytes 3072 | tf_op jit(solution)/shard_map/all_gather | solution.py:16
  325.5 6.7 %all-gather.47 = f32[4,1,256]{2,1,0:T(1,128)S(1)} all-gather(f32[1,1,256]{2,1,0:T(1,128)S(1)} %bitcast.233), channel_id=20, replica_groups=mesh['strip_0'=8,'strip_1'=2,'sample_0'=4,'sample_1'=4] {'sample_0'}, dimensions={0}, use_global_device_ids=true | all-gather | bytes 5120 | tf_op jit(solution)/shard_map/all_gather | solution.py:16
  332.2 5.5 all-gather.48
  339.3 18.1 %all-gather.53 = f32[8,4,256]{2,1,0:T(4,128)S(1)} all-gather(f32[1,4,256]{2,1,0:T(4,128)S(1)} %maximum_bitcast_fusion), channel_id=26, replica_groups=mesh['strip_0'=8,'strip_1'=2,'sample_0'=4,'sample_1'=4] {'strip_0'}, dimensions={0}, use_global_device_ids=true | all-gather | bytes 36864 | tf_op jit(solution)/shard_map/all_gather | solution.py:16
  357.4 12.2 %all-gather.54 = f32[2,4,256]{2,1,0:T(4,128)S(1)} all-gather(f32[1,4,256]{2,1,0:T(4,128)S(1)} %bitcast.196), channel_id=27, replica_groups=mesh['strip_0'=8,'strip_1'=2,'sample_0'=4,'sample_1'=4] {'strip_1'}, dimensions={0}, use_global_device_ids=true | all-gather | bytes 12288 | tf_op jit(solution)/shard_map/all_gather | solution.py:16
  369.7 9.0 %all-gather.55 = f32[4,4,256]{2,1,0:T(4,128)S(1)} all-gather(f32[1,4,256]{2,1,0:T(4,128)S(1)} %bitcast.197), channel_id=28, replica_groups=mesh['strip_0'=8,'strip_1'=2,'sample_0'=4,'sample_1'=4] {'sample_0'}, dimensions={0}, use_global_device_ids=true | all-gather | bytes 20480 | tf_op jit(solution)/shard_map/all_gather | solution.py:16
  378.7 9.0 %all-gather.56 = f32[4,4,256]{2,1,0:T(4,128)S(1)} all-gather(f32[1,4,256]{2,1,0:T(4,128)S(1)} %bitcast.198), channel_id=29, replica_groups=mesh['strip_0'=8,'strip_1'=2,'sample_0'=4,'sample_1'=4] {'sample_1'}, dimensions={0}, use_global_device_ids=true | all-gather | bytes 20480 | tf_op jit(solution)/shard_map/all_gather | solution.py:16
  388.0 2.6 collective-permute-start.3
  390.6 1.3 collective-permute-start.2
  392.5 14.5 %all-to-all-start.1 = ((f32[16,1,256]{2,1,0:T(1,128)}), f32[16,1,256]{2,1,0:T(1,128)S(1)}, u32[]{:S(2)}, u32[]{:S(2)}) async-start(f32[16,1,256]{2,1,0:T(1,128)} %broadcast_in_dim.12), calls=%async_computation.1 | async-start | bytes 32768 | tf_op jit(solution)/shard_map/all_to_all | solution.py:29
  408.1 6.2 %all-to-all-done.1 = f32[16,1,256]{2,1,0:T(1,128)S(1)} async-done(((f32[16,1,256]{2,1,0:T(1,128)}), f32[16,1,256]{2,1,0:T(1,128)S(1)}, u32[]{:S(2)}, u32[]{:S(2)}) %all-to-all-start.1) | async-done | bytes 16416 | tf_op jit(solution)/shard_map/all_to_all | solution.py:29
  424.5 2.7 reshape.112
  427.2 7.6 %fusion = bf16[2048,2560]{0,1:T(8,128)(2,1)S(1)} fusion(bf16[324,2560]{1,0:T(8,128)(2,1)} %reshape.112, bf16[324,2048]{0,1:T(8,128)(2,1)} %bitcast.184), kind=kOutput, calls=%fused_computation.2 | convolution fusion | flops 3407872000 | bytes 13471744 | tf_op jit(solution)/shard_map/dot_general | solution.py:258
  434.8 11.3 %pad_maximum_fusion = bf16[2048,2816]{0,1:T(8,128)(2,1)} fusion(bf16[2048,256]{0,1:T(8,128)(2,1)S(1)} %multiply_convert_fusion.1, bf16[2048,2560]{0,1:T(8,128)(2,1)S(1)} %fusion), kind=kLoop, calls=%fused_computation.1 | loop fusion | flops 23068672 | bytes 23068672 | tf_op jit(solution)/shard_map/concatenate | solution.py:264
  446.2 15.3 %copy.30 = bf16[2048,2816]{1,0:T(8,128)(2,1)} copy(bf16[2048,2816]{0,1:T(8,128)(2,1)} %pad_maximum_fusion) | data formatting | bytes 23068672
  461.8 67.4 %reduce-scatter.4.cloned.1.call-done = bf16[128,2816]{1,0:T(8,128)(2,1)} async-done(((bf16[2048,2816]{1,0:T(8,128)(2,1)}), bf16[128,2816]{1,0:T(8,128)(2,1)}) %reduce-scatter.4.cloned.1.call-update) | async-done | bytes 720912 | tf_op jit(solution)/shard_map/reduce_scatter | solution.py:263
  529.2 6.4 %all-to-all-start.2 = ((bf16[16,8,2816]{2,1,0:T(8,128)(2,1)}), bf16[16,8,2816]{2,1,0:T(8,128)(2,1)S(1)}, u32[]{:S(2)}, u32[]{:S(2)}) async-start(bf16[16,8,2816]{2,1,0:T(8,128)(2,1)} %bitcast.186), calls=%async_computation.2 | async-start | bytes 1441792 | tf_op jit(solution)/shard_map/all_to_all | solution.py:51
  536.5 1.6 fusion.12
  538.1 8.0 %all-to-all-done.2 = bf16[16,8,2816]{2,1,0:T(8,128)(2,1)S(1)} async-done(((bf16[16,8,2816]{2,1,0:T(8,128)(2,1)}), bf16[16,8,2816]{2,1,0:T(8,128)(2,1)S(1)}, u32[]{:S(2)}, u32[]{:S(2)}) %all-to-all-start.2) | async-done | bytes 720928 | tf_op jit(solution)/shard_map/all_to_all | solution.py:51
  546.1 4.2 all-to-all-start.4
  550.3 2.0 convolution_add_fusion
  552.3 1.3 reduce_sum.513
  553.6 4.9 all-to-all-done.4
  559.4 10.6 %all-to-all-start.3 = ((bf16[16,8,2816]{2,1,0:T(8,128)(2,1)}), bf16[16,8,2816]{2,1,0:T(8,128)(2,1)}, u32[]{:S(2)}, u32[]{:S(2)}) async-start(bf16[16,8,2816]{2,1,0:T(8,128)(2,1)} %broadcast_in_dim.14), calls=%async_computation.3 | async-start | bytes 1441792 | tf_op jit(solution)/shard_map/all_to_all | solution.py:29
  570.1 3.3 fusion.3
  573.5 3.2 convolution_add_fusion.2
  576.7 4.3 fusion.2
  582.1 19.0 %all-gather.28 = bf16[768,256]{1,0:T(8,128)(2,1)S(1)} all-gather(bf16[48,256]{1,0:T(8,128)(2,1)S(1)} %reduce_sum.514), channel_id=30, replica_groups=mesh['strip_0'=8,'strip_1'=2,'sample_0'=4,'sample_1'=4] {'strip_0','stri..., dimensions={0}, use_global_device_ids=true | all-gather | bytes 417792 | tf_op jit(solution)/shard_map/all_gather | solution.py:67
  601.8 1.2 bitcast_convert_fusion
  (137 shorter events, 24.1 us)
Async XLA Ops:
  7.2 2.2 copy-start.1
  7.2 97.9 %all-gather.59.cloned.1.call-start = ((), (), s32[]{:S(2)}) async-start(), calls=%async_computation.6 | async-start | bytes 12255232 | tf_op jit(solution)/shard_map/all_gather | solution.py:23
  10.3 44.2 %all-to-all-start = ((f32[16,1,2048]{2,1,0:T(1,128)}), f32[16,1,2048]{2,1,0:T(1,128)}, u32[]{:S(2)}, u32[]{:S(2)}) async-start(f32[16,1,2048]{2,1,0:T(1,128)} %broadcast_in_dim.10), calls=%async_computation | async-start | bytes 262144 | tf_op jit(solution)/shard_map/all_to_all | solution.py:29
  20.3 92.2 %collective-permute-start.1 = (bf16[3,108,2048]{2,1,0:T(8,128)(2,1)S(1)}, bf16[3,108,2048]{2,1,0:T(8,128)(2,1)}, u32[]{:S(2)}, u32[]{:S(2)}) collective-permute-start(bf16[3,108,2048]{2,1,0:T(8,128)(2,1)S(1)} %bitcast.182), channel_id=1, source_target_pairs={{0,64},{16,80},{32,96},{48,112},{64,128},{80,144},{96,160},{112,17... | collective-permute-start | bytes 3981320 | tf_op jit(solution)/shard_map/ppermute | solution.py:41
  25.6 91.5 %collective-permute-start = (bf16[3,108,2048]{2,1,0:T(8,128)(2,1)S(1)}, bf16[3,108,2048]{2,1,0:T(8,128)(2,1)}, u32[]{:S(2)}, u32[]{:S(2)}) collective-permute-start(bf16[3,108,2048]{2,1,0:T(8,128)(2,1)S(1)} %bitcast.183), channel_id=1, source_target_pairs={{64,0},{80,16},{96,32},{112,48},{128,64},{144,80},{160,96},{176,11... | collective-permute-start | bytes 3981320 | tf_op jit(solution)/shard_map/ppermute | solution.py:41
  31.0 2.8 copy-start.17
  54.5 284.2 %copy-start.10 = (bf16[768,256]{1,0:T(8,128)(2,1)}, bf16[768,256]{1,0:T(8,128)(2,1)S(1)}, u32[]{:S(2)}) copy-start(bf16[768,256]{1,0:T(8,128)(2,1)S(1)} %all_gather.191) | copy-start | bytes 1179652
  109.2 5.2 copy-start
  120.6 296.8 %copy-start.2 = (f32[256,3,108]{0,2,1:T(8,128)}, f32[256,3,108]{0,2,1:T(8,128)S(1)}, u32[]{:S(2)}) copy-start(f32[256,3,108]{0,2,1:T(8,128)S(1)} %get-tuple-element.61) | copy-start | bytes 995332
  120.6 152.6 %copy-start.13 = (bf16[1,3,108,256]{3,2,1,0:T(8,128)(2,1)S(1)}, bf16[1,3,108,256]{3,2,1,0:T(8,128)(2,1)}, u32[]{:S(2)}) copy-start(bf16[1,3,108,256]{3,2,1,0:T(8,128)(2,1)} %param.11) | copy-start | bytes 497668
  388.0 33.4 %copy-start.6 = (bf16[3,108,256]{2,1,0:T(8,128)(2,1)}, bf16[3,108,256]{2,1,0:T(8,128)(2,1)S(1)}, u32[]{:S(2)}) copy-start(bf16[3,108,256]{2,1,0:T(8,128)(2,1)S(1)} %multiply_convert_fusion.2) | copy-start | bytes 497668
  388.0 34.2 %collective-permute-start.3 = (bf16[3,108,256]{2,1,0:T(8,128)(2,1)S(1)}, bf16[3,108,256]{2,1,0:T(8,128)(2,1)S(1)}, u32[]{:S(2)}, u32[]{:S(2)}) collective-permute-start(bf16[3,108,256]{2,1,0:T(8,128)(2,1)S(1)} %multiply_convert_fusion.2), channel_id=1, source_target_pairs={{0,64},{16,80},{32,96},{48,112},{64,128},{80,144},{96,160},{112,17... | collective-permute-start | bytes 497672 | tf_op jit(solution)/shard_map/ppermute | solution.py:41
  390.6 27.0 %collective-permute-start.2 = (bf16[3,108,256]{2,1,0:T(8,128)(2,1)S(1)}, bf16[3,108,256]{2,1,0:T(8,128)(2,1)S(1)}, u32[]{:S(2)}, u32[]{:S(2)}) collective-permute-start(bf16[3,108,256]{2,1,0:T(8,128)(2,1)S(1)} %multiply_convert_fusion.2), channel_id=1, source_target_pairs={{64,0},{80,16},{96,32},{112,48},{128,64},{144,80},{160,96},{176,11... | collective-permute-start | bytes 497672 | tf_op jit(solution)/shard_map/ppermute | solution.py:41
  392.5 21.8 %all-to-all-start.1 = ((f32[16,1,256]{2,1,0:T(1,128)}), f32[16,1,256]{2,1,0:T(1,128)S(1)}, u32[]{:S(2)}, u32[]{:S(2)}) async-start(f32[16,1,256]{2,1,0:T(1,128)} %broadcast_in_dim.12), calls=%async_computation.1 | async-start | bytes 32768 | tf_op jit(solution)/shard_map/all_to_all | solution.py:29
  407.0 122.2 %reduce-scatter.4.cloned.1.call-start = ((), (), s32[]{:S(2)}) async-start(), calls=%async_computation.7 | async-start | bytes 12255232 | tf_op jit(solution)/shard_map/reduce_scatter | solution.py:263
  417.6 9.6 %copy-start.4 = (bf16[3,108,256]{2,1,0:T(8,128)(2,1)}, bf16[3,108,256]{2,1,0:T(8,128)(2,1)S(1)}, u32[]{:S(2)}) copy-start(bf16[3,108,256]{2,1,0:T(8,128)(2,1)S(1)} %collective-permute-done.2) | copy-start | bytes 497668
  422.2 5.0 copy-start.8
  529.2 16.9 %all-to-all-start.2 = ((bf16[16,8,2816]{2,1,0:T(8,128)(2,1)}), bf16[16,8,2816]{2,1,0:T(8,128)(2,1)S(1)}, u32[]{:S(2)}, u32[]{:S(2)}) async-start(bf16[16,8,2816]{2,1,0:T(8,128)(2,1)} %bitcast.186), calls=%async_computation.2 | async-start | bytes 1441792 | tf_op jit(solution)/shard_map/all_to_all | solution.py:51
  546.1 4.2 copy-start.3
  546.1 12.5 %all-to-all-start.4 = ((bf16[16,48,256]{2,1,0:T(8,128)(2,1)}), bf16[16,48,256]{2,1,0:T(8,128)(2,1)}, u32[]{:S(2)}, u32[]{:S(2)}) async-start(bf16[16,48,256]{2,1,0:T(8,128)(2,1)} %bitcast.69), calls=%async_computation.4 | async-start | bytes 786432 | tf_op jit(solution)/shard_map/all_to_all | solution.py:51
  552.3 17.8 %copy-start.7 = (bf16[3,108,256]{2,1,0:T(8,128)(2,1)S(1)}, bf16[3,108,256]{2,1,0:T(8,128)(2,1)}, u32[]{:S(2)}) copy-start(bf16[3,108,256]{2,1,0:T(8,128)(2,1)} %copy-done.6) | copy-start | bytes 497668
  552.3 17.8 %copy-start.16 = (bf16[3,108,256]{2,1,0:T(8,128)(2,1)S(1)}, bf16[3,108,256]{2,1,0:T(8,128)(2,1)}, u32[]{:S(2)}) copy-start(bf16[3,108,256]{2,1,0:T(8,128)(2,1)} %get-tuple-element.44) | copy-start | bytes 497668
  559.4 42.3 %all-to-all-start.3 = ((bf16[16,8,2816]{2,1,0:T(8,128)(2,1)}), bf16[16,8,2816]{2,1,0:T(8,128)(2,1)}, u32[]{:S(2)}, u32[]{:S(2)}) async-start(bf16[16,8,2816]{2,1,0:T(8,128)(2,1)} %broadcast_in_dim.14), calls=%async_computation.3 | async-start | bytes 1441792 | tf_op jit(solution)/shard_map/all_to_all | solution.py:29
  570.1 3.3 copy-start.5
  570.1 3.3 copy-start.11
  570.1 3.3 copy-start.12
  573.5 3.2 copy-start.9
  573.5 3.2 copy-start.14
  573.5 3.2 copy-start.15
Sparse Core Ops, SparseCore 0:
  11.0 94.0 all-gather.58
  461.6 67.5 reduce-scatter.3
